TPU v7x, 256 devices: a whole 4x4x8 slice. The times are simulated.
256 devices in a mesh: vessel: 2 (over core), gather: 128 (over y, x, z).
Axes of the slice: x: 4, y: 4, z: 8, core: 2. Of those that a mesh axis runs over, the one named last changes fastest.
Arguments:
- observed: bfloat16 [128, 128, 2048], P('gather'), may hold values from -6 to 6
- estimate: bfloat16 [2, 128, 128, 2048], P('vessel', 'gather'), may hold values from -6 to 6
- delays: int32 [2, 128], P('vessel', 'gather'), may hold values from 0 to 256
- taps_time: float32 [16, 7], replicated, may hold values from -2 to 2
- taps_shot: float32 [16, 7], replicated, may hold values from -0.5 to 0.5
- thresh: float32 [16], replicated, may hold values from 0.02 to 0.3
Outputs:
- deblended: bfloat16 [2, 128, 128, 2048], P('vessel', 'gather')
All inputs are finite; a program needn't handle non-finite values.
Results may differ from a plain program's by a relative error of at most 0.022.
Values may be sent and summed in bfloat16 or wider, within the bound.
No kernel may reach another device: no remote copies, remote signals or barrier semaphores. Data moves between devices by JAX's collectives and lax.ppermute only.
A program may use at most 64 MiB of HBM per device.

v0:
```python
import functools

import jax
import jax.numpy as jnp
import numpy as np
from jax import lax
from jax.experimental import pallas as pl
from jax.experimental.pallas import tpu as pltpu
from jax.sharding import Mesh, PartitionSpec as P

ITERS = 2
TT = 2048
TILES = TT // 128
HALF = TILES // 2
REC = 128
PAIR = 64
BLOCK = 32
CH = 16
TAPS = 7
STEP = 4
ROWS = CH * BLOCK
COLS = 256
HALO = TAPS * BLOCK
WIDE = TT + 128
TILE = 256
UNROLL = 4


def column_tables():
    tap = np.full((2, COLS), -1, np.int32)
    shot = np.full((2, COLS), -1000, np.int32)
    for block in range(2):
        for k in range(TAPS):
            tap[block, k * BLOCK : (k + 1) * BLOCK] = k
            shot[block, k * BLOCK : (k + 1) * BLOCK] = np.arange(BLOCK)
            at = HALO + 4 * k
            tap[block, at : at + 4] = k
            shot[block, at : at + 4] = np.arange(4) + (BLOCK if block == 0 else -4)
    return tap, shot


def filter_matrices(taps_time, taps_shot):
    tap, shot = column_tables()
    offset = shot[:, None, :] - np.arange(BLOCK)[None, :, None] + 3
    time_part = sum(
        jnp.where(tap[:, None, None, :] == k, taps_time[None, :, None, None, k], 0.0) for k in range(TAPS)
    )
    shot_part = sum(
        jnp.where(offset[:, None] == j, taps_shot[None, :, None, None, j], 0.0) for j in range(TAPS)
    )
    forward = (time_part * shot_part).astype(jnp.bfloat16).reshape(2, ROWS, COLS)
    return forward, forward.transpose(0, 2, 1)


def to_messages(half_ref, x_ref, obs_ref, out_ref, wide_ref):
    for j in range(TILES):
        wide_ref[:, j, :] = x_ref[:, 128 * j : 128 * (j + 1)].astype(jnp.float32)
    for j in range(HALF):
        at = pl.multiple_of((half_ref[0] * HALF + j) * 128, 128)
        wide_ref[:, TILES + j, :] = obs_ref[:, pl.ds(at, 128)].astype(jnp.float32)
    out_ref[...] = wide_ref[...].astype(jnp.bfloat16)


def from_messages(in_ref, out_ref, wide_ref):
    wide_ref[...] = in_ref[...].astype(jnp.float32)
    for j in range(TILES):
        out_ref[:, 128 * j : 128 * (j + 1)] = wide_ref[:, j, :].astype(jnp.bfloat16)


def pack(current, observed, vessel):
    step = 32
    return pl.pallas_call(
        to_messages,
        out_shape=jax.ShapeDtypeStruct((REC, TILES + HALF, 128), jnp.bfloat16),
        grid_spec=pltpu.PrefetchScalarGridSpec(
            num_scalar_prefetch=1,
            grid=(REC // step,),
            in_specs=[
                pl.BlockSpec((step, TT), lambda i, _: (i, 0)),
                pl.BlockSpec((step, TT), lambda i, _: (i, 0)),
            ],
            out_specs=pl.BlockSpec((step, TILES + HALF, 128), lambda i, _: (i, 0, 0)),
            scratch_shapes=[pltpu.VMEM((step, TILES + HALF, 128), jnp.float32)],
        ),
        name="pack",
    )(vessel, current, observed)


def unpack(messages):
    step = 32
    return pl.pallas_call(
        from_messages,
        out_shape=jax.ShapeDtypeStruct((REC, TT), jnp.bfloat16),
        grid=(REC // step,),
        in_specs=[pl.BlockSpec((step, TILES, 128), lambda i: (i, 0, 0))],
        out_specs=pl.BlockSpec((step, TT), lambda i: (i, 0)),
        scratch_shapes=[pltpu.VMEM((step, TILES, 128), jnp.float32)],
        name="unpack",
    )(messages)


def late(x, delay, slot, lane):
    part, whole = delay & 127, delay >> 7
    slot[8:24, :] = pltpu.roll(x, part, 1)
    near = slot[pl.ds(8 - whole, 16), :]
    far = slot[pl.ds(7 - whole, 16), :]
    return jnp.where(lane >= part, near, far)


def early(x, delay, slot, lane):
    part, whole = delay & 127, delay >> 7
    slot[0:16, :] = pltpu.roll(x, (128 - part) & 127, 1)
    near = slot[pl.ds(whole, 16), :]
    far = slot[pl.ds(whole + 1, 16), :]
    return jnp.where(lane < 128 - part, near, far)


def deblend_kernel(
    delays_ref, thresh_ref, recv_ref, fwd_ref, bwd_ref, out_ref,
    traces, observed, planes, wide, columns, halo, shrunk, spread, *slots
):
    lane = lax.broadcasted_iota(jnp.int32, (TILES, 128), 1)
    row = lax.broadcasted_iota(jnp.int32, (8, TT), 0)

    traces[...] = recv_ref[:, :TILES, :].astype(jnp.float32)
    observed[:, :HALF, :] = recv_ref[:PAIR, TILES:, :].astype(jnp.float32)
    observed[:, HALF:, :] = recv_ref[PAIR:, TILES:, :].astype(jnp.float32)
    for slot in slots:
        slot[...] = jnp.zeros_like(slot)
    wide[:, TT:] = jnp.zeros((PAIR, 128), jnp.float32)
    spread[:, :, TT:] = jnp.zeros((2, COLS, 128), jnp.float32)
    halo[...] = jnp.zeros_like(halo)

    def one_iteration(_, carry):
        def blend_some(group, carry):
            for u in range(UNROLL):
                shot = group * UNROLL + u
                first, second = delays_ref[shot], delays_ref[PAIR + shot]
                mine = slots[4 * u : 4 * u + 4]
                a, b = traces[shot], traces[PAIR + shot]
                resid = observed[shot] - (late(a, first, mine[0], lane) + late(b, second, mine[1], lane))
                planes[0, shot] = a + early(resid, first, mine[2], lane)
                planes[1, shot] = b + early(resid, second, mine[3], lane)
            return carry

        lax.fori_loop(0, PAIR // UNROLL, blend_some, 0)

        def one_vessel(vessel, carry):
            for j in range(TILES):
                wide[:, 128 * j : 128 * (j + 1)] = planes[vessel, :, j, :]
            for g in range(PAIR // 16):
                rows = wide[16 * g : 16 * g + 16, :]
                block, inner = g // 2, 16 * (g % 2)
                for k in range(TAPS):
                    moved = rows if k == 3 else pltpu.roll(rows, (STEP * (3 - k)) % WIDE, 1)
                    moved = moved[:, :TT]
                    columns[block, k * BLOCK + inner : k * BLOCK + inner + 16, :] = moved.astype(jnp.bfloat16)
                    if g == 2:
                        halo[0, 4 * k : 4 * k + 4, :] = moved[0:4]
                    if g == 1:
                        halo[1, 4 * k : 4 * k + 4, :] = moved[12:16]
            columns[:, HALO:, :] = halo[...].astype(jnp.bfloat16)

            def one_tile(n, carry):
                at = pl.ds(pl.multiple_of(n * TILE, TILE), TILE)
                for block in range(2):
                    piece = columns[block, :, at]
                    for c4 in range(CH // 4):
                        y = jnp.dot(
                            fwd_ref[block, 128 * c4 : 128 * (c4 + 1), :], piece,
                            preferred_element_type=jnp.float32,
                        )
                        for c in range(4):
                            limit = thresh_ref[4 * c4 + c]
                            part = y[BLOCK * c : BLOCK * (c + 1)]
                            z = part - jnp.clip(part, -limit, limit)
                            start = 128 * c4 + BLOCK * c
                            shrunk[block, start : start + BLOCK, :] = z.astype(jnp.bfloat16)
                    spread[block, :, at] = jnp.dot(
                        bwd_ref[block], shrunk[block], preferred_element_type=jnp.float32
                    )
                return carry

            lax.fori_loop(0, TT // TILE, one_tile, 0)

            for block in range(2):
                for g in range(BLOCK // 8):
                    total = None
                    for k in range(TAPS):
                        part = spread[block, k * BLOCK + 8 * g : k * BLOCK + 8 * g + 8, :]
                        if k != 3:
                            part = pltpu.roll(part, (STEP * (k - 3)) % WIDE, 1)
                        part = part[:, :TT]
                        total = part if total is None else total + part
                    edge = 3 if block == 0 else 0
                    if g == edge:
                        even = odd = None
                        for m in range(4):
                            pair = spread[1 - block, HALO + 8 * m : HALO + 8 * m + 8, :]
                            moved = pltpu.roll(pair, (STEP * (2 * m - 3)) % WIDE, 1)[:, :TT]
                            even = moved if even is None else even + moved
                            if m < 3:
                                moved = pltpu.roll(pair, (STEP * (2 * m - 2)) % WIDE, 1)[:, :TT]
                                odd = moved if odd is None else odd + moved
                        if block == 0:
                            total = total + jnp.where(row >= 4, pltpu.roll(even, 4, 0) + odd, 0.0)
                        else:
                            total = total + jnp.where(row < 4, even + pltpu.roll(odd, 4, 0), 0.0)
                    total = total.astype(jnp.bfloat16).astype(jnp.float32)
                    at = pl.ds(vessel * PAIR + block * BLOCK + 8 * g, 8)
                    for j in range(TILES):
                        traces[at, j, :] = total[:, 128 * j : 128 * (j + 1)]
            return carry

        lax.fori_loop(0, 2, one_vessel, 0)
        return carry

    lax.fori_loop(0, ITERS, one_iteration, 0)
    out_ref[...] = traces[...].astype(jnp.bfloat16)


def deblend(delays, thresh, messages, forward, backward):
    vmem = pl.BlockSpec(memory_space=pltpu.VMEM)
    smem = pl.BlockSpec(memory_space=pltpu.SMEM)
    f32 = jnp.float32
    return pl.pallas_call(
        deblend_kernel,
        out_shape=jax.ShapeDtypeStruct((REC, TILES, 128), jnp.bfloat16),
        in_specs=[smem, smem, vmem, vmem, vmem],
        out_specs=vmem,
        scratch_shapes=[
            pltpu.VMEM((REC, TILES, 128), f32),
            pltpu.VMEM((PAIR, TILES, 128), f32),
            pltpu.VMEM((2, PAIR, TILES, 128), f32),
            pltpu.VMEM((PAIR, WIDE), f32),
            pltpu.VMEM((2, COLS, TT), jnp.bfloat16),
            pltpu.VMEM((2, BLOCK, TT), f32),
            pltpu.VMEM((2, ROWS, TILE), jnp.bfloat16),
            pltpu.VMEM((2, COLS, WIDE), f32),
        ]
        + [pltpu.VMEM((24, 128), f32)] * (4 * UNROLL),
        compiler_params=pltpu.CompilerParams(vmem_limit_bytes=40 << 20),
        name="deblend",
    )(delays, thresh, messages, forward, backward)


def per_device(observed, estimate, delays, taps_time, taps_shot, thresh):
    group = ("vessel", "pairs")
    vessel = lax.axis_index("vessel").reshape(1).astype(jnp.int32)
    sent = pack(estimate[0, 0], observed[0], vessel)
    all_delays = lax.all_gather(delays.reshape(1), group, tiled=True)
    messages = lax.all_to_all(sent, group, split_axis=0, concat_axis=0, tiled=True)
    forward, backward = filter_matrices(taps_time, taps_shot)
    result = deblend(all_delays, thresh, messages, forward, backward)
    back = lax.all_to_all(result, group, split_axis=0, concat_axis=0, tiled=True)
    return unpack(back)[None, None]


def solution(mesh):
    split = Mesh(mesh.devices.reshape(2, PAIR, 2), ("vessel", "pairs", "parity"))
    shots = ("pairs", "parity")
    return jax.shard_map(
        per_device,
        mesh=split,
        in_specs=(
            P(shots, None, None),
            P("vessel", shots, None, None),
            P("vessel", shots),
            P(),
            P(),
            P(),
        ),
        out_specs=P("vessel", shots, None, None),
        check_vma=False,
    )
```

profile of v0, /device:TPU:1, one launch (start us, length us, event | category | flops | bytes accessed | tf_op | source)
XLA Modules:
  0.0 130.6 jit_solution(9990360311700350997)
XLA Ops:
  0.0 3.8 %pack.1 = bf16[128,24,128]{2,1,0:T(8,128)(2,1)} custom-call(s32[1]{0:T(128)} %bitcast.2.half_ref, bf16[128,2048]{1,0:T(8,128)(2,1)} %bitcast.53, bf16[128,2048]{1,0:T(8,128)(2,1)} %bitcast.54), custom_call_target="tpu_custom_call" | custom-call | tf_op jit(solution)/shard_map/pack/pallas_call | solution.py:72
  3.9 16.9 %all-to-all-start = ((bf16[128,24,128]{2,1,0:T(8,128)(2,1)}), bf16[128,24,128]{2,1,0:T(8,128)(2,1)S(1)}, u32[]{:S(2)}, u32[]{:S(2)}) async-start(bf16[128,24,128]{2,1,0:T(8,128)(2,1)} %pack.1), calls=%async_computation | async-start | bytes 1572864 | tf_op jit(solution)/shard_map/all_to_all | solution.py:252
  20.8 0.6 copy-done.10
  21.4 0.1 select_add_fusion
  21.6 0.3 copy.29
  22.0 0.3 copy-done.9
  22.4 0.1 broadcast_in_dim.307
  22.5 0.1 broadcast_in_dim.315
  22.7 0.1 broadcast_in_dim.322
  22.8 0.1 broadcast_in_dim.329
  23.1 0.1 broadcast_in_dim.343
  23.4 0.7 copy-done.7
  24.1 0.4 copy.22
  24.5 0.3 copy-done.6
  24.9 0.4 copy.23
  25.3 0.3 copy-done.5
  25.7 0.4 copy.24
  26.1 0.3 copy-done.4
  26.5 0.4 copy.25
  26.9 0.3 copy-done.3
  27.4 1.1 copy.26
  28.5 1.0 copy.27
  29.7 1.0 copy.28
  30.7 2.1 %multiply_convert_fusion = bf16[2,512,256]{1,2,0:T(8,128)(2,1)S(1)} fusion(f32[2,512,256]{1,2,0:T(8,128)S(1)} %copy.29, pred[2,512,256]{1,2,0:T(8,128)(4,1)} %copy.28, pred[2,512,256]{1,2,0:T(8,128)(4,1)} %copy.27, pred[2,512,256]{1,2,0:T(8,128)(4,1)} %copy.26, pred[2,512,256]{1,2,0:T(8,128)(4,1)S(1)} %copy.25, pred[2,512,256]{1,2,0:T(8,128)(4,1)S(1)} %copy.24, ...), kind=kLoop, calls=%fused_computation | loop fusion | flops 3932160 | bytes 3422208 | tf_op jit(solution)/shard_map/convert_element_type | solution.py:51
  32.8 0.2 copy.30.fwd_ref
  33.7 0.6 dynamic-slice
  34.3 0.7 bitcast_dynamic-update-slice_fusion
  35.0 28.1 %all-reduce.delays_ref = s32[128]{0:T(128)S(1)} all-reduce(s32[128]{0:T(128)S(1)} %bitcast_dynamic-update-slice_fusion), channel_id=2, replica_groups=mesh['vessel'=2,'pairs'=64,'parity'=2] {'vessel','pairs'}, use_global_device_ids=true, to_apply=%add | all-reduce | flops 128 | bytes 1024 | tf_op jit(solution)/shard_map/all_gather | solution.py:251
  63.1 0.7 copy-done
  63.8 38.1 %deblend.1 = bf16[128,16,128]{2,1,0:T(8,128)(2,1)S(1)} custom-call(s32[128]{0:T(128)S(1)} %all-reduce.delays_ref, f32[16]{0:T(128)S(1)} %copy-done, bf16[128,24,128]{2,1,0:T(8,128)(2,1)S(1)} %all-to-all-done.recv_ref, bf16[2,512,256]{2,1,0:T(8,128)(2,1)S(1)} %copy.30.fwd_ref, bf16[2,256,512]{2,1,0:T(8,128)(2,1)S(1)} %bitcast.44), custom_call_target="tpu_custom_call" | custom-call | tf_op jit(solution)/shard_map/deblend/pallas_call | solution.py:226
  101.8 25.1 %all_to_all.10.in_ref = bf16[128,16,128]{2,1,0:T(8,128)(2,1)} all-to-all(bf16[128,16,128]{2,1,0:T(8,128)(2,1)S(1)} %deblend.1), channel_id=1, replica_groups=mesh['vessel'=2,'pairs'=64,'parity'=2] {'vessel','pairs'}, dimensions={0} | all-to-all | bytes 1048576 | tf_op jit(solution)/shard_map/all_to_all | solution.py:255
  126.9 3.7 %unpack.1 = bf16[128,2048]{1,0:T(8,128)(2,1)} custom-call(bf16[128,16,128]{2,1,0:T(8,128)(2,1)} %all_to_all.10.in_ref), custom_call_target="tpu_custom_call" | custom-call | tf_op jit(solution)/shard_map/unpack/pallas_call | solution.py:91
  (56 shorter events, 1.4 us)
Async XLA Ops:
  3.8 16.9 %copy-start.8 = (f32[16,7]{0,1:T(8,128)S(1)}, f32[16,7]{0,1:T(8,128)}, u32[]{:S(2)}) copy-start(f32[16,7]{0,1:T(8,128)} %param.23) | copy-start | bytes 1348
  3.8 17.0 %copy-start.11 = (pred[2,256]{1,0:T(4,128)(4,1)S(1)}, pred[2,256]{1,0:T(4,128)(4,1)}, u32[]{:S(2)}) copy-start(pred[2,256]{1,0:T(4,128)(4,1)} %constant.54) | copy-start | bytes 1540
  3.8 17.0 %copy-start.12 = (pred[2,256]{1,0:T(4,128)(4,1)S(1)}, pred[2,256]{1,0:T(4,128)(4,1)}, u32[]{:S(2)}) copy-start(pred[2,256]{1,0:T(4,128)(4,1)} %constant.55) | copy-start | bytes 1540
  3.8 17.0 %copy-start.13 = (pred[2,256]{1,0:T(4,128)(4,1)S(1)}, pred[2,256]{1,0:T(4,128)(4,1)}, u32[]{:S(2)}) copy-start(pred[2,256]{1,0:T(4,128)(4,1)} %constant.56) | copy-start | bytes 1540
  3.8 17.0 %copy-start.14 = (pred[2,256]{1,0:T(4,128)(4,1)S(1)}, pred[2,256]{1,0:T(4,128)(4,1)}, u32[]{:S(2)}) copy-start(pred[2,256]{1,0:T(4,128)(4,1)} %constant.57) | copy-start | bytes 1540
  3.8 17.0 %copy-start.15 = (pred[2,256]{1,0:T(4,128)(4,1)S(1)}, pred[2,256]{1,0:T(4,128)(4,1)}, u32[]{:S(2)}) copy-start(pred[2,256]{1,0:T(4,128)(4,1)} %constant.58) | copy-start | bytes 1540
  3.8 17.0 %copy-start.16 = (pred[2,256]{1,0:T(4,128)(4,1)S(1)}, pred[2,256]{1,0:T(4,128)(4,1)}, u32[]{:S(2)}) copy-start(pred[2,256]{1,0:T(4,128)(4,1)} %constant.59) | copy-start | bytes 1540
  3.9 59.2 %all-to-all-start = ((bf16[128,24,128]{2,1,0:T(8,128)(2,1)}), bf16[128,24,128]{2,1,0:T(8,128)(2,1)S(1)}, u32[]{:S(2)}, u32[]{:S(2)}) async-start(bf16[128,24,128]{2,1,0:T(8,128)(2,1)} %pack.1), calls=%async_computation | async-start | bytes 1572864 | tf_op jit(solution)/shard_map/all_to_all | solution.py:252
  20.8 0.7 copy-start.10
  21.6 0.7 copy-start.9
  23.3 0.7 copy-start.7
  24.1 0.7 copy-start.6
  24.9 0.7 copy-start.5
  25.7 0.7 copy-start.4
  26.5 0.7 copy-start.3
  27.3 1.1 copy-start.2
  28.5 1.1 copy-start.1
  33.0 0.7 copy-start.17
  63.1 0.7 copy-start
where the time goes:
time: 131 us
  blocking collectives  53.2 us (41%)
  Pallas kernels  45.5 us (35%)
  starting transfers between devices  16.9 us (13%)
  local copies, waits for them, and re-layouts  11.8 us (9%)
  other arithmetic  2.16 us (2%)
    pallas_call x1, Pallas kernels, deblend(): pl.pallas_call(deblend_kernel, out_shape=jax.ShapeDtypeStruct((REC, TILES...  38.1 us
    all_gather x1, blocking collectives, per_device(): all_delays = lax.all_gather(delays.reshape(1), group, tiled=True)  28.1 us
    all_to_all x1, blocking collectives, per_device(): lax.all_to_all(result, group, split_axis=0, concat_axis=0, tiled=True)  25.1 us
    all_to_all x1, starting transfers between devices, per_device(): lax.all_to_all(sent, group, split_axis=0, concat_axis=0, tiled=True)  16.9 us
    broadcast_in_dim x29, local copies, waits for them, and re-layouts, filter_matrices(): jnp.where(offset[:, None] == j, taps_shot[None, :, None, None, j], 0.0)  6.29 us
    unnamed x46, local copies, waits for them, and re-layouts  4.93 us
    pallas_call x1, Pallas kernels, pack(): pl.pallas_call(to_messages, out_shape=jax.ShapeDtypeStruct((REC, TILES +...  3.79 us
    pallas_call x1, Pallas kernels, unpack(): pl.pallas_call(from_messages, out_shape=jax.ShapeDtypeStruct((REC, TT), j...  3.7 us
  transfers between devices with their start and end apart: 1, of which 0 were waited for; matrix products, arithmetic and copies ran while one was open for 8% of the time, Pallas kernels for 0%

commit v1 on v0

--- a/solution.py
+++ b/solution.py
@@ -22,8 +22,9 @@
 COLS = 256
 HALO = TAPS * BLOCK
 WIDE = TT + 128
+ITEM = TILES + HALF + 2
 TILE = 256
-UNROLL = 4
+UNROLL = 8
 
 
 def column_tables():
@@ -52,12 +53,16 @@
     return forward, forward.transpose(0, 2, 1)
 
 
-def to_messages(half_ref, x_ref, obs_ref, out_ref, wide_ref):
+def to_messages(half_ref, delay_ref, x_ref, obs_ref, out_ref, wide_ref):
+    rows = x_ref.shape[0]
     for j in range(TILES):
-        wide_ref[:, j, :] = x_ref[:, 128 * j : 128 * (j + 1)].astype(jnp.float32)
+        wide_ref[pl.ds(j, rows, stride=ITEM), :] = x_ref[:, 128 * j : 128 * (j + 1)].astype(jnp.float32)
     for j in range(HALF):
         at = pl.multiple_of((half_ref[0] * HALF + j) * 128, 128)
-        wide_ref[:, TILES + j, :] = obs_ref[:, pl.ds(at, 128)].astype(jnp.float32)
+        wide_ref[pl.ds(TILES + j, rows, stride=ITEM), :] = obs_ref[:, pl.ds(at, 128)].astype(jnp.float32)
+    delay = jnp.full((rows, 128), delay_ref[0].astype(jnp.float32), jnp.float32)
+    for j in range(TILES + HALF, ITEM):
+        wide_ref[pl.ds(j, rows, stride=ITEM), :] = delay
     out_ref[...] = wide_ref[...].astype(jnp.bfloat16)
 
 
@@ -67,23 +72,23 @@
         out_ref[:, 128 * j : 128 * (j + 1)] = wide_ref[:, j, :].astype(jnp.bfloat16)
 
 
-def pack(current, observed, vessel):
+def pack(current, observed, vessel, delay):
     step = 32
     return pl.pallas_call(
         to_messages,
-        out_shape=jax.ShapeDtypeStruct((REC, TILES + HALF, 128), jnp.bfloat16),
+        out_shape=jax.ShapeDtypeStruct((REC * ITEM, 128), jnp.bfloat16),
         grid_spec=pltpu.PrefetchScalarGridSpec(
-            num_scalar_prefetch=1,
+            num_scalar_prefetch=2,
             grid=(REC // step,),
             in_specs=[
-                pl.BlockSpec((step, TT), lambda i, _: (i, 0)),
-                pl.BlockSpec((step, TT), lambda i, _: (i, 0)),
+                pl.BlockSpec((step, TT), lambda i, *_: (i, 0)),
+                pl.BlockSpec((step, TT), lambda i, *_: (i, 0)),
             ],
-            out_specs=pl.BlockSpec((step, TILES + HALF, 128), lambda i, _: (i, 0, 0)),
-            scratch_shapes=[pltpu.VMEM((step, TILES + HALF, 128), jnp.float32)],
+            out_specs=pl.BlockSpec((step * ITEM, 128), lambda i, *_: (i, 0)),
+            scratch_shapes=[pltpu.VMEM((step * ITEM, 128), jnp.float32)],
         ),
         name="pack",
-    )(vessel, current, observed)
+    )(vessel, delay, current, observed)
 
 
 def unpack(messages):
@@ -116,26 +121,42 @@
 
 
 def deblend_kernel(
-    delays_ref, thresh_ref, recv_ref, fwd_ref, bwd_ref, out_ref,
-    traces, observed, planes, wide, columns, halo, shrunk, spread, *slots
+    thresh_ref, recv_ref, fwd_ref, bwd_ref, out_ref,
+    arrived, delay_row, delays_ref, arrival, traces, observed, planes, wide, columns, halo, shrunk, spread, *slots
 ):
     lane = lax.broadcasted_iota(jnp.int32, (TILES, 128), 1)
     row = lax.broadcasted_iota(jnp.int32, (8, TT), 0)
 
-    traces[...] = recv_ref[:, :TILES, :].astype(jnp.float32)
-    observed[:, :HALF, :] = recv_ref[:PAIR, TILES:, :].astype(jnp.float32)
-    observed[:, HALF:, :] = recv_ref[PAIR:, TILES:, :].astype(jnp.float32)
+    arrived[...] = recv_ref[...].astype(jnp.float32)
+    by_message = arrived[pl.ds(TILES + HALF, REC, stride=ITEM), :].astype(jnp.int32)
+    square = lax.broadcasted_iota(jnp.int32, (REC, 128), 0) == lax.broadcasted_iota(jnp.int32, (REC, 128), 1)
+    delay_row[...] = jnp.sum(jnp.where(square, by_message, 0), axis=0, keepdims=True)
+    fetch = pltpu.make_async_copy(delay_row, delays_ref, arrival)
+    fetch.start()
+
+    def sort_out(group, carry):
+        for u in range(8):
+            at = group * (8 * ITEM) + u * ITEM
+            shot = group * 8 + u
+            traces[shot] = arrived[pl.ds(at, TILES), :]
+            traces[PAIR + shot] = arrived[pl.ds(at + PAIR * ITEM, TILES), :]
+            observed[shot, :HALF, :] = arrived[pl.ds(at + TILES, HALF), :]
+            observed[shot, HALF:, :] = arrived[pl.ds(at + PAIR * ITEM + TILES, HALF), :]
+        return carry
+
+    lax.fori_loop(0, PAIR // 8, sort_out, 0)
     for slot in slots:
         slot[...] = jnp.zeros_like(slot)
     wide[:, TT:] = jnp.zeros((PAIR, 128), jnp.float32)
     spread[:, :, TT:] = jnp.zeros((2, COLS, 128), jnp.float32)
     halo[...] = jnp.zeros_like(halo)
+    fetch.wait()
 
     def one_iteration(_, carry):
         def blend_some(group, carry):
             for u in range(UNROLL):
                 shot = group * UNROLL + u
-                first, second = delays_ref[shot], delays_ref[PAIR + shot]
+                first, second = delays_ref[0, shot], delays_ref[0, PAIR + shot]
                 mine = slots[4 * u : 4 * u + 4]
                 a, b = traces[shot], traces[PAIR + shot]
                 resid = observed[shot] - (late(a, first, mine[0], lane) + late(b, second, mine[1], lane))
@@ -165,23 +186,18 @@
                 at = pl.ds(pl.multiple_of(n * TILE, TILE), TILE)
                 for block in range(2):
                     piece = columns[block, :, at]
-                    for c4 in range(CH // 4):
-                        y = jnp.dot(
-                            fwd_ref[block, 128 * c4 : 128 * (c4 + 1), :], piece,
-                            preferred_element_type=jnp.float32,
-                        )
-                        for c in range(4):
-                            limit = thresh_ref[4 * c4 + c]
-                            part = y[BLOCK * c : BLOCK * (c + 1)]
-                            z = part - jnp.clip(part, -limit, limit)
-                            start = 128 * c4 + BLOCK * c
-                            shrunk[block, start : start + BLOCK, :] = z.astype(jnp.bfloat16)
+                    y = jnp.dot(fwd_ref[block], piece, preferred_element_type=jnp.float32)
+                    for c in range(CH):
+                        limit = thresh_ref[c]
+                        part = y[BLOCK * c : BLOCK * (c + 1)]
+                        z = part - jnp.clip(part, -limit, limit)
+                        shrunk[block, BLOCK * c : BLOCK * (c + 1), :] = z.astype(jnp.bfloat16)
                     spread[block, :, at] = jnp.dot(
                         bwd_ref[block], shrunk[block], preferred_element_type=jnp.float32
                     )
                 return carry
 
-            lax.fori_loop(0, TT // TILE, one_tile, 0)
+            lax.fori_loop(0, TT // TILE, one_tile, 0, unroll=True)
 
             for block in range(2):
                 for g in range(BLOCK // 8):
@@ -212,23 +228,27 @@
                         traces[at, j, :] = total[:, 128 * j : 128 * (j + 1)]
             return carry
 
-        lax.fori_loop(0, 2, one_vessel, 0)
+        lax.fori_loop(0, 2, one_vessel, 0, unroll=True)
         return carry
 
     lax.fori_loop(0, ITERS, one_iteration, 0)
     out_ref[...] = traces[...].astype(jnp.bfloat16)
 
 
-def deblend(delays, thresh, messages, forward, backward):
+def deblend(thresh, messages, forward, backward):
     vmem = pl.BlockSpec(memory_space=pltpu.VMEM)
     smem = pl.BlockSpec(memory_space=pltpu.SMEM)
     f32 = jnp.float32
     return pl.pallas_call(
         deblend_kernel,
         out_shape=jax.ShapeDtypeStruct((REC, TILES, 128), jnp.bfloat16),
-        in_specs=[smem, smem, vmem, vmem, vmem],
+        in_specs=[smem, vmem, vmem, vmem],
         out_specs=vmem,
         scratch_shapes=[
+            pltpu.VMEM((REC * ITEM, 128), f32),
+            pltpu.VMEM((1, 128), jnp.int32),
+            pltpu.SMEM((1, 128), jnp.int32),
+            pltpu.SemaphoreType.DMA,
             pltpu.VMEM((REC, TILES, 128), f32),
             pltpu.VMEM((PAIR, TILES, 128), f32),
             pltpu.VMEM((2, PAIR, TILES, 128), f32),
@@ -241,17 +261,17 @@
         + [pltpu.VMEM((24, 128), f32)] * (4 * UNROLL),
         compiler_params=pltpu.CompilerParams(vmem_limit_bytes=40 << 20),
         name="deblend",
-    )(delays, thresh, messages, forward, backward)
+    )(thresh, messages, forward, backward)
 
 
 def per_device(observed, estimate, delays, taps_time, taps_shot, thresh):
     group = ("vessel", "pairs")
     vessel = lax.axis_index("vessel").reshape(1).astype(jnp.int32)
-    sent = pack(estimate[0, 0], observed[0], vessel)
-    all_delays = lax.all_gather(delays.reshape(1), group, tiled=True)
+    sent = pack(estimate[0, 0], observed[0], vessel, delays.reshape(1))
+    sent = sent.reshape(REC, ITEM // 2, 2, 128)
     messages = lax.all_to_all(sent, group, split_axis=0, concat_axis=0, tiled=True)
     forward, backward = filter_matrices(taps_time, taps_shot)
-    result = deblend(all_delays, thresh, messages, forward, backward)
+    result = deblend(thresh, messages.reshape(REC * ITEM, 128), forward, backward)
     back = lax.all_to_all(result, group, split_axis=0, concat_axis=0, tiled=True)
     return unpack(back)[None, None]
 

time: 131 us -> 94 us (0.72)
  blocking collectives: 53.2 us -> 26.8 us
  Pallas kernels: 45.5 us -> 22.6 us
  waiting for transfers between devices: 0.01 us -> 13.3 us
    all_gather x1 -> x0, blocking collectives: 28.1 us -> none  [per_device(): all_delays = lax.all_gather(delays.reshape(1), group, tiled=True)]
    pallas_call x1, Pallas kernels: 38.1 us -> 15.5 us  [deblend(): pl.pallas_call(deblend_kernel, out_shape=jax.ShapeDtypeStruct((REC, TILES...]
    all_to_all x1, waiting for transfers between devices: 0.01 us -> 13.3 us  [per_device(): lax.all_to_all(sent, group, split_axis=0, concat_axis=0, tiled=True)]
    all_to_all x1, blocking collectives: 25.1 us -> 26.8 us  [per_device(): lax.all_to_all(result, group, split_axis=0, concat_axis=0, tiled=True)]
    unnamed x46 -> x41, local copies, waits for them, and re-layouts: 4.93 us -> 3.66 us
  transfers between devices with their start and end apart: 1 -> 1, of which waited for: 0 -> 1; matrix products, arithmetic and copies ran while one was open for 8% -> 10% of each run, Pallas kernels for 0% -> 0%
where the time goes in v1:
time: 94 us; the launch traced here: 93.2 us
  blocking collectives  26.8 us (29%)
  Pallas kernels  22.6 us (24%)
  starting transfers between devices  16.9 us (18%)
  waiting for transfers between devices  13.3 us (14%)
  local copies, waits for them, and re-layouts  10.6 us (11%)
  other arithmetic  2.16 us (2%)
    all_to_all x1, blocking collectives, per_device(): lax.all_to_all(result, group, split_axis=0, concat_axis=0, tiled=True)  26.8 us
    all_to_all x1, starting transfers between devices, per_device(): lax.all_to_all(sent, group, split_axis=0, concat_axis=0, tiled=True)  16.9 us
    pallas_call x1, Pallas kernels, deblend(): pl.pallas_call(deblend_kernel, out_shape=jax.ShapeDtypeStruct((REC, TILES...  15.5 us
    all_to_all x1, waiting for transfers between devices, per_device(): lax.all_to_all(sent, group, split_axis=0, concat_axis=0, tiled=True)  13.3 us
    broadcast_in_dim x29, local copies, waits for them, and re-layouts, filter_matrices(): jnp.where(offset[:, None] == j, taps_shot[None, :, None, None, j], 0.0)  6.28 us
    pallas_call x1, Pallas kernels, unpack(): pl.pallas_call(from_messages, out_shape=jax.ShapeDtypeStruct((REC, TT), j...  3.7 us
    unnamed x41, local copies, waits for them, and re-layouts  3.66 us
    pallas_call x1, Pallas kernels, pack(): pl.pallas_call(to_messages, out_shape=jax.ShapeDtypeStruct((REC * ITEM, 1...  3.43 us
  transfers between devices with their start and end apart: 1, of which 1 were waited for; matrix products, arithmetic and copies ran while one was open for 10% of the time, Pallas kernels for 0%

profile of v1, /device:TPU:1, one launch (start us, length us, event | category | flops | bytes accessed | tf_op | source)
XLA Modules:
  0.0 93.2 jit_solution(6376083590826098534)
XLA Ops:
  0.7 3.4 %pack.1 = bf16[3328,128]{1,0:T(8,128)(2,1)} custom-call(s32[1]{0:T(128)} %bitcast.half_ref, s32[1]{0:T(128)} %bitcast.44.delay_ref, bf16[128,2048]{1,0:T(8,128)(2,1)} %bitcast.56, bf16[128,2048]{1,0:T(8,128)(2,1)} %bitcast.57), custom_call_target="tpu_custom_call" | custom-call | tf_op jit(solution)/shard_map/pack/pallas_call | solution.py:77
  4.1 16.9 %all-to-all-start = ((bf16[128,13,2,128]{3,2,1,0:T(2,128)(2,1)}), bf16[128,13,2,128]{3,2,1,0:T(2,128)(2,1)S(1)}, u32[]{:S(2)}, u32[]{:S(2)}) async-start(bf16[128,13,2,128]{3,2,1,0:T(2,128)(2,1)} %bitcast.48), calls=%async_computation | async-start | bytes 1703936 | tf_op jit(solution)/shard_map/all_to_all | solution.py:272
  21.1 0.6 copy-done.10
  21.7 0.1 select_add_fusion
  21.9 0.3 copy.29
  22.2 0.3 copy-done.9
  22.7 0.1 broadcast_in_dim.307
  22.8 0.1 broadcast_in_dim.315
  23.0 0.1 broadcast_in_dim.322
  23.1 0.1 broadcast_in_dim.329
  23.3 0.1 broadcast_in_dim.336
  23.4 0.1 broadcast_in_dim.343
  23.6 0.1 broadcast_in_dim.350
  23.6 0.7 copy-done.7
  24.4 0.4 copy.22
  24.8 0.3 copy-done.6
  25.2 0.4 copy.23
  25.6 0.3 copy-done.5
  26.0 0.4 copy.24
  26.4 0.3 copy-done.4
  26.8 0.4 copy.25
  27.2 0.3 copy-done.3
  27.6 1.0 %copy.26 = pred[2,512,256]{1,2,0:T(8,128)(4,1)} copy(pred[2,512,256]{2,1,0:T(8,128)(4,1)S(1)} %bitcast.53) | data formatting | bytes 524288 | tf_op jit(solution)/shard_map/jit(_where)/broadcast_in_dim | solution.py:50
  28.8 1.1 %copy.27 = pred[2,512,256]{1,2,0:T(8,128)(4,1)} copy(pred[2,512,256]{2,1,0:T(8,128)(4,1)S(1)} %bitcast.54) | data formatting | bytes 524288 | tf_op jit(solution)/shard_map/jit(_where)/broadcast_in_dim | solution.py:50
  29.9 1.0 %copy.28 = pred[2,512,256]{1,2,0:T(8,128)(4,1)} copy(pred[2,512,256]{2,1,0:T(8,128)(4,1)S(1)} %bitcast.55) | data formatting | bytes 524288 | tf_op jit(solution)/shard_map/jit(_where)/broadcast_in_dim | solution.py:50
  31.0 2.1 %multiply_convert_fusion = bf16[2,512,256]{1,2,0:T(8,128)(2,1)S(1)} fusion(f32[2,512,256]{1,2,0:T(8,128)S(1)} %copy.29, pred[2,512,256]{1,2,0:T(8,128)(4,1)} %copy.28, pred[2,512,256]{1,2,0:T(8,128)(4,1)} %copy.27, pred[2,512,256]{1,2,0:T(8,128)(4,1)} %copy.26, pred[2,512,256]{1,2,0:T(8,128)(4,1)S(1)} %copy.25, pred[2,512,256]{1,2,0:T(8,128)(4,1)S(1)} %copy.24, ...), kind=kLoop, calls=%fused_computation | loop fusion | flops 3932160 | bytes 3422208 | tf_op jit(solution)/shard_map/convert_element_type | solution.py:52
  33.1 0.2 copy.30.fwd_ref
  33.3 13.3 %all-to-all-done = bf16[128,13,2,128]{3,2,1,0:T(2,128)(2,1)S(1)} async-done(((bf16[128,13,2,128]{3,2,1,0:T(2,128)(2,1)}), bf16[128,13,2,128]{3,2,1,0:T(2,128)(2,1)S(1)}, u32[]{:S(2)}, u32[]{:S(2)}) %all-to-all-start) | async-done | bytes 852000 | tf_op jit(solution)/shard_map/all_to_all | solution.py:272
  46.6 0.7 copy-done
  47.3 15.5 %deblend.1 = bf16[128,16,128]{2,1,0:T(8,128)(2,1)S(1)} custom-call(f32[16]{0:T(128)S(1)} %copy-done, bf16[3328,128]{1,0:T(8,128)(2,1)S(1)} %bitcast.46, bf16[2,512,256]{2,1,0:T(8,128)(2,1)S(1)} %copy.30.fwd_ref, bf16[2,256,512]{2,1,0:T(8,128)(2,1)S(1)} %bitcast.45), custom_call_target="tpu_custom_call" | custom-call | tf_op jit(solution)/shard_map/deblend/pallas_call | solution.py:242
  62.8 26.8 %all_to_all.10.in_ref = bf16[128,16,128]{2,1,0:T(8,128)(2,1)} all-to-all(bf16[128,16,128]{2,1,0:T(8,128)(2,1)S(1)} %deblend.1), channel_id=1, replica_groups=mesh['vessel'=2,'pairs'=64,'parity'=2] {'vessel','pairs'}, dimensions={0} | all-to-all | bytes 1048576 | tf_op jit(solution)/shard_map/all_to_all | solution.py:275
  89.5 3.7 %unpack.1 = bf16[128,2048]{1,0:T(8,128)(2,1)} custom-call(bf16[128,16,128]{2,1,0:T(8,128)(2,1)} %all_to_all.10.in_ref), custom_call_target="tpu_custom_call" | custom-call | tf_op jit(solution)/shard_map/unpack/pallas_call | solution.py:96
  (50 shorter events, 1.2 us)
Async XLA Ops:
  4.1 16.9 %copy-start.8 = (f32[16,7]{0,1:T(8,128)S(1)}, f32[16,7]{0,1:T(8,128)}, u32[]{:S(2)}) copy-start(f32[16,7]{0,1:T(8,128)} %param.23) | copy-start | bytes 1348
  4.1 17.0 %copy-start.11 = (pred[2,256]{1,0:T(4,128)(4,1)S(1)}, pred[2,256]{1,0:T(4,128)(4,1)}, u32[]{:S(2)}) copy-start(pred[2,256]{1,0:T(4,128)(4,1)} %constant.54) | copy-start | bytes 1540
  4.1 17.0 %copy-start.12 = (pred[2,256]{1,0:T(4,128)(4,1)S(1)}, pred[2,256]{1,0:T(4,128)(4,1)}, u32[]{:S(2)}) copy-start(pred[2,256]{1,0:T(4,128)(4,1)} %constant.55) | copy-start | bytes 1540
  4.1 17.0 %copy-start.13 = (pred[2,256]{1,0:T(4,128)(4,1)S(1)}, pred[2,256]{1,0:T(4,128)(4,1)}, u32[]{:S(2)}) copy-start(pred[2,256]{1,0:T(4,128)(4,1)} %constant.56) | copy-start | bytes 1540
  4.1 17.0 %copy-start.14 = (pred[2,256]{1,0:T(4,128)(4,1)S(1)}, pred[2,256]{1,0:T(4,128)(4,1)}, u32[]{:S(2)}) copy-start(pred[2,256]{1,0:T(4,128)(4,1)} %constant.57) | copy-start | bytes 1540
  4.1 17.0 %copy-start.15 = (pred[2,256]{1,0:T(4,128)(4,1)S(1)}, pred[2,256]{1,0:T(4,128)(4,1)}, u32[]{:S(2)}) copy-start(pred[2,256]{1,0:T(4,128)(4,1)} %constant.58) | copy-start | bytes 1540
  4.1 17.0 %copy-start.16 = (pred[2,256]{1,0:T(4,128)(4,1)S(1)}, pred[2,256]{1,0:T(4,128)(4,1)}, u32[]{:S(2)}) copy-start(pred[2,256]{1,0:T(4,128)(4,1)} %constant.59) | copy-start | bytes 1540
  4.1 42.5 %all-to-all-start = ((bf16[128,13,2,128]{3,2,1,0:T(2,128)(2,1)}), bf16[128,13,2,128]{3,2,1,0:T(2,128)(2,1)S(1)}, u32[]{:S(2)}, u32[]{:S(2)}) async-start(bf16[128,13,2,128]{3,2,1,0:T(2,128)(2,1)} %bitcast.48), calls=%async_computation | async-start | bytes 1703936 | tf_op jit(solution)/shard_map/all_to_all | solution.py:272
  21.0 0.7 copy-start.10
  21.9 0.7 copy-start.9
  23.6 0.7 copy-start.7
  24.4 0.7 copy-start.6
  25.2 0.7 copy-start.5
  26.0 0.7 copy-start.4
  26.8 0.7 copy-start.3
  27.6 1.1 %copy-start.2 = (pred[2,32,256]{2,1,0:T(32,128)(4,1)S(1)}, pred[2,32,256]{2,1,0:T(32,128)(4,1)}, u32[]{:S(2)}) copy-start(pred[2,32,256]{2,1,0:T(32,128)(4,1)} %constant.65) | copy-start | bytes 49156
  28.8 1.1 %copy-start.1 = (pred[2,32,256]{2,1,0:T(32,128)(4,1)S(1)}, pred[2,32,256]{2,1,0:T(32,128)(4,1)}, u32[]{:S(2)}) copy-start(pred[2,32,256]{2,1,0:T(32,128)(4,1)} %constant.66) | copy-start | bytes 49156
  46.6 0.7 copy-start

commit v2 on v1

--- a/solution.py
+++ b/solution.py
@@ -2,7 +2,6 @@
 
 import jax
 import jax.numpy as jnp
-import numpy as np
 from jax import lax
 from jax.experimental import pallas as pl
 from jax.experimental.pallas import tpu as pltpu
@@ -24,82 +23,134 @@
 WIDE = TT + 128
 ITEM = TILES + HALF + 2
 TILE = 256
+PART = 32
 UNROLL = 8
 
 
-def column_tables():
-    tap = np.full((2, COLS), -1, np.int32)
-    shot = np.full((2, COLS), -1000, np.int32)
+def filter_matrices(time_ref, shot_ref, fwd_ref, bwd_ref):
+    lane = lax.broadcasted_iota(jnp.int32, (CH, ROWS), 1)
+    chosen = jnp.where(lane // BLOCK == lax.broadcasted_iota(jnp.int32, (CH, ROWS), 0), 1.0, 0.0)
+    spread_out = functools.partial(
+        jnp.dot, precision=lax.Precision.HIGHEST, preferred_element_type=jnp.float32
+    )
+    time_taps = spread_out(time_ref[...], chosen)
+    shot_taps = spread_out(shot_ref[...], chosen)
+
+    def shot_part(shot, shape):
+        offset = shot - lax.broadcasted_iota(jnp.int32, shape, 1) % BLOCK + 3
+        total = jnp.zeros(shape, jnp.float32)
+        for j in range(TAPS):
+            total = jnp.where(offset == j, shot_taps[j : j + 1], total)
+        return total
+
+    own = shot_part(lax.broadcasted_iota(jnp.int32, (BLOCK, ROWS), 0), (BLOCK, ROWS))
+    main = jnp.concatenate([own * time_taps[k : k + 1] for k in range(TAPS)], axis=0)
+    row = lax.broadcasted_iota(jnp.int32, (8, ROWS), 0)
     for block in range(2):
-        for k in range(TAPS):
-            tap[block, k * BLOCK : (k + 1) * BLOCK] = k
-            shot[block, k * BLOCK : (k + 1) * BLOCK] = np.arange(BLOCK)
-            at = HALO + 4 * k
-            tap[block, at : at + 4] = k
-            shot[block, at : at + 4] = np.arange(4) + (BLOCK if block == 0 else -4)
-    return tap, shot
-
-
-def filter_matrices(taps_time, taps_shot):
-    tap, shot = column_tables()
-    offset = shot[:, None, :] - np.arange(BLOCK)[None, :, None] + 3
-    time_part = sum(
-        jnp.where(tap[:, None, None, :] == k, taps_time[None, :, None, None, k], 0.0) for k in range(TAPS)
-    )
-    shot_part = sum(
-        jnp.where(offset[:, None] == j, taps_shot[None, :, None, None, j], 0.0) for j in range(TAPS)
-    )
-    forward = (time_part * shot_part).astype(jnp.bfloat16).reshape(2, ROWS, COLS)
-    return forward, forward.transpose(0, 2, 1)
-
-
-def to_messages(half_ref, delay_ref, x_ref, obs_ref, out_ref, wide_ref):
-    rows = x_ref.shape[0]
-    for j in range(TILES):
-        wide_ref[pl.ds(j, rows, stride=ITEM), :] = x_ref[:, 128 * j : 128 * (j + 1)].astype(jnp.float32)
-    for j in range(HALF):
-        at = pl.multiple_of((half_ref[0] * HALF + j) * 128, 128)
-        wide_ref[pl.ds(TILES + j, rows, stride=ITEM), :] = obs_ref[:, pl.ds(at, 128)].astype(jnp.float32)
-    delay = jnp.full((rows, 128), delay_ref[0].astype(jnp.float32), jnp.float32)
-    for j in range(TILES + HALF, ITEM):
-        wide_ref[pl.ds(j, rows, stride=ITEM), :] = delay
-    out_ref[...] = wide_ref[...].astype(jnp.bfloat16)
-
-
-def from_messages(in_ref, out_ref, wide_ref):
-    wide_ref[...] = in_ref[...].astype(jnp.float32)
-    for j in range(TILES):
-        out_ref[:, 128 * j : 128 * (j + 1)] = wide_ref[:, j, :].astype(jnp.bfloat16)
-
-
-def pack(current, observed, vessel, delay):
-    step = 32
+        near = shot_part(row % 4 + (BLOCK if block == 0 else -4), (8, ROWS))
+        groups = []
+        for m in range(4):
+            late_tap = time_taps[2 * m + 1 : 2 * m + 2] if m < 3 else jnp.zeros((1, ROWS), jnp.float32)
+            groups.append(near * jnp.where(row < 4, time_taps[2 * m : 2 * m + 1], late_tap))
+        both = jnp.concatenate([main] + groups, axis=0)
+        bwd_ref[block] = both.astype(jnp.bfloat16)
+        fwd_ref[block] = both.T.astype(jnp.bfloat16)
+
+
+def to_messages(
+    half_ref, delay_ref, x_hbm, obs_hbm, time_hbm, shot_hbm, out_ref, fwd_ref, bwd_ref,
+    x_ref, obs_ref, time_ref, shot_ref, wide_ref, arrivals, taps_arrivals,
+):
+    taps = [
+        pltpu.make_async_copy(time_hbm, time_ref, taps_arrivals.at[0]),
+        pltpu.make_async_copy(shot_hbm, shot_ref, taps_arrivals.at[1]),
+    ]
+    copies = []
+    for part in range(REC // PART):
+        rows = pl.ds(PART * part, PART)
+        columns = pl.ds(pl.multiple_of(half_ref[0] * (TT // 2), TT // 2), TT // 2)
+        copies.append(pltpu.make_async_copy(x_hbm.at[rows], x_ref.at[rows], arrivals.at[2 * part]))
+        copies.append(pltpu.make_async_copy(obs_hbm.at[rows, columns], obs_ref.at[rows], arrivals.at[2 * part + 1]))
+    for copy in taps + copies:
+        copy.start()
+    for copy in taps:
+        copy.wait()
+    filter_matrices(time_ref, shot_ref, fwd_ref, bwd_ref)
+    delay = jnp.full((PART, 128), delay_ref[0].astype(jnp.float32), jnp.float32)
+    for part in range(REC // PART):
+        base = part * PART * ITEM
+        rows = pl.ds(PART * part, PART)
+        copies[2 * part].wait()
+        for j in range(TILES):
+            wide_ref[pl.ds(base + j, PART, stride=ITEM), :] = x_ref[rows, 128 * j : 128 * (j + 1)].astype(jnp.float32)
+        copies[2 * part + 1].wait()
+        for j in range(HALF):
+            wide_ref[pl.ds(base + TILES + j, PART, stride=ITEM), :] = obs_ref[
+                rows, 128 * j : 128 * (j + 1)
+            ].astype(jnp.float32)
+        for j in range(TILES + HALF, ITEM):
+            wide_ref[pl.ds(base + j, PART, stride=ITEM), :] = delay
+        done = pl.ds(base, PART * ITEM)
+        out_ref[done, :] = wide_ref[done, :].astype(jnp.bfloat16)
+
+
+def from_messages(in_ref, out_hbm, wide_ref, out_ref, departures):
+    copies = []
+    for part in range(REC // PART):
+        rows = pl.ds(PART * part, PART)
+        wide_ref[rows] = in_ref[rows].astype(jnp.float32)
+        for j in range(TILES):
+            out_ref[rows, 128 * j : 128 * (j + 1)] = wide_ref[rows, j, :].astype(jnp.bfloat16)
+        copies.append(pltpu.make_async_copy(out_ref.at[rows], out_hbm.at[rows], departures.at[part]))
+        copies[-1].start()
+    for copy in copies:
+        copy.wait()
+
+
+def stay(value):
+    return pltpu.with_memory_space_constraint(value, pltpu.HBM)
+
+
+def pack(current, observed, vessel, delay, taps_time, taps_shot):
+    vmem = pl.BlockSpec(memory_space=pltpu.VMEM)
+    smem = pl.BlockSpec(memory_space=pltpu.SMEM)
+    hbm = pl.BlockSpec(memory_space=pltpu.HBM)
+    bf16 = jnp.bfloat16
     return pl.pallas_call(
         to_messages,
-        out_shape=jax.ShapeDtypeStruct((REC * ITEM, 128), jnp.bfloat16),
-        grid_spec=pltpu.PrefetchScalarGridSpec(
-            num_scalar_prefetch=2,
-            grid=(REC // step,),
-            in_specs=[
-                pl.BlockSpec((step, TT), lambda i, *_: (i, 0)),
-                pl.BlockSpec((step, TT), lambda i, *_: (i, 0)),
-            ],
-            out_specs=pl.BlockSpec((step * ITEM, 128), lambda i, *_: (i, 0)),
-            scratch_shapes=[pltpu.VMEM((step * ITEM, 128), jnp.float32)],
+        out_shape=(
+            jax.ShapeDtypeStruct((REC * ITEM, 128), bf16),
+            jax.ShapeDtypeStruct((2, ROWS, COLS), bf16),
+            jax.ShapeDtypeStruct((2, COLS, ROWS), bf16),
         ),
+        in_specs=[smem, smem, hbm, hbm, hbm, hbm],
+        out_specs=(vmem, vmem, vmem),
+        scratch_shapes=[
+            pltpu.VMEM((REC, TT), bf16),
+            pltpu.VMEM((REC, TT // 2), bf16),
+            pltpu.VMEM((TAPS, CH), jnp.float32),
+            pltpu.VMEM((TAPS, CH), jnp.float32),
+            pltpu.VMEM((REC * ITEM, 128), jnp.float32),
+            pltpu.SemaphoreType.DMA((2 * REC // PART,)),
+            pltpu.SemaphoreType.DMA((2,)),
+        ],
+        compiler_params=pltpu.CompilerParams(vmem_limit_bytes=16 << 20),
         name="pack",
-    )(vessel, delay, current, observed)
+    )(vessel, delay, *(stay(value) for value in (current, observed, taps_time, taps_shot)))
 
 
 def unpack(messages):
-    step = 32
     return pl.pallas_call(
         from_messages,
         out_shape=jax.ShapeDtypeStruct((REC, TT), jnp.bfloat16),
-        grid=(REC // step,),
-        in_specs=[pl.BlockSpec((step, TILES, 128), lambda i: (i, 0, 0))],
-        out_specs=pl.BlockSpec((step, TT), lambda i: (i, 0)),
-        scratch_shapes=[pltpu.VMEM((step, TILES, 128), jnp.float32)],
+        in_specs=[pl.BlockSpec(memory_space=pltpu.VMEM)],
+        out_specs=pl.BlockSpec(memory_space=pltpu.HBM),
+        scratch_shapes=[
+            pltpu.VMEM((REC, TILES, 128), jnp.float32),
+            pltpu.VMEM((REC, TT), jnp.bfloat16),
+            pltpu.SemaphoreType.DMA((REC // PART,)),
+        ],
+        compiler_params=pltpu.CompilerParams(vmem_limit_bytes=16 << 20),
         name="unpack",
     )(messages)
 
@@ -121,17 +172,19 @@
 
 
 def deblend_kernel(
-    thresh_ref, recv_ref, fwd_ref, bwd_ref, out_ref,
-    arrived, delay_row, delays_ref, arrival, traces, observed, planes, wide, columns, halo, shrunk, spread, *slots
+    thresh_hbm, recv_ref, fwd_ref, bwd_ref, out_ref,
+    thresh_ref, arrived, delay_row, delays_ref, arrivals, traces, observed, planes, wide, columns, halo, shrunk, spread, *slots
 ):
     lane = lax.broadcasted_iota(jnp.int32, (TILES, 128), 1)
     row = lax.broadcasted_iota(jnp.int32, (8, TT), 0)
 
+    limits = pltpu.make_async_copy(thresh_hbm, thresh_ref, arrivals.at[1])
+    limits.start()
     arrived[...] = recv_ref[...].astype(jnp.float32)
     by_message = arrived[pl.ds(TILES + HALF, REC, stride=ITEM), :].astype(jnp.int32)
     square = lax.broadcasted_iota(jnp.int32, (REC, 128), 0) == lax.broadcasted_iota(jnp.int32, (REC, 128), 1)
     delay_row[...] = jnp.sum(jnp.where(square, by_message, 0), axis=0, keepdims=True)
-    fetch = pltpu.make_async_copy(delay_row, delays_ref, arrival)
+    fetch = pltpu.make_async_copy(delay_row, delays_ref, arrivals.at[0])
     fetch.start()
 
     def sort_out(group, carry):
@@ -151,6 +204,7 @@
     spread[:, :, TT:] = jnp.zeros((2, COLS, 128), jnp.float32)
     halo[...] = jnp.zeros_like(halo)
     fetch.wait()
+    limits.wait()
 
     def one_iteration(_, carry):
         def blend_some(group, carry):
@@ -237,18 +291,19 @@
 
 def deblend(thresh, messages, forward, backward):
     vmem = pl.BlockSpec(memory_space=pltpu.VMEM)
-    smem = pl.BlockSpec(memory_space=pltpu.SMEM)
+    hbm = pl.BlockSpec(memory_space=pltpu.HBM)
     f32 = jnp.float32
     return pl.pallas_call(
         deblend_kernel,
         out_shape=jax.ShapeDtypeStruct((REC, TILES, 128), jnp.bfloat16),
-        in_specs=[smem, vmem, vmem, vmem],
+        in_specs=[hbm, vmem, vmem, vmem],
         out_specs=vmem,
         scratch_shapes=[
+            pltpu.SMEM((CH,), f32),
             pltpu.VMEM((REC * ITEM, 128), f32),
             pltpu.VMEM((1, 128), jnp.int32),
             pltpu.SMEM((1, 128), jnp.int32),
-            pltpu.SemaphoreType.DMA,
+            pltpu.SemaphoreType.DMA((2,)),
             pltpu.VMEM((REC, TILES, 128), f32),
             pltpu.VMEM((PAIR, TILES, 128), f32),
             pltpu.VMEM((2, PAIR, TILES, 128), f32),
@@ -261,16 +316,17 @@
         + [pltpu.VMEM((24, 128), f32)] * (4 * UNROLL),
         compiler_params=pltpu.CompilerParams(vmem_limit_bytes=40 << 20),
         name="deblend",
-    )(thresh, messages, forward, backward)
+    )(stay(thresh), messages, forward, backward)
 
 
 def per_device(observed, estimate, delays, taps_time, taps_shot, thresh):
     group = ("vessel", "pairs")
     vessel = lax.axis_index("vessel").reshape(1).astype(jnp.int32)
-    sent = pack(estimate[0, 0], observed[0], vessel, delays.reshape(1))
+    sent, forward, backward = pack(
+        estimate[0, 0], observed[0], vessel, delays.reshape(1), taps_time.T, taps_shot.T
+    )
     sent = sent.reshape(REC, ITEM // 2, 2, 128)
     messages = lax.all_to_all(sent, group, split_axis=0, concat_axis=0, tiled=True)
-    forward, backward = filter_matrices(taps_time, taps_shot)
     result = deblend(thresh, messages.reshape(REC * ITEM, 128), forward, backward)
     back = lax.all_to_all(result, group, split_axis=0, concat_axis=0, tiled=True)
     return unpack(back)[None, None]

time: 94 us -> 88.2 us (0.938)
  blocking collectives: 26.8 us -> 68.8 us
  starting transfers between devices: 16.9 us -> 0 us
  waiting for transfers between devices: 13.3 us -> 0 us
  local copies, waits for them, and re-layouts: 10.6 us -> 0 us
  Pallas kernels: 22.6 us -> 18.5 us
  other arithmetic: 2.16 us -> 0 us
    all_to_all x0 -> x1, blocking collectives: none -> 42.1 us  [per_device(): lax.all_to_all(sent, group, split_axis=0, concat_axis=0, tiled=True)]
    all_to_all x1 -> x0, starting transfers between devices: 16.9 us -> none  [per_device(): lax.all_to_all(sent, group, split_axis=0, concat_axis=0, tiled=True)]
    all_to_all x1 -> x0, waiting for transfers between devices: 13.3 us -> none  [per_device(): lax.all_to_all(sent, group, split_axis=0, concat_axis=0, tiled=True)]
    broadcast_in_dim x30 -> x0, local copies, waits for them, and re-layouts: 6.29 us -> none  [the longest x29 6.28 us: filter_matrices(): jnp.where(offset[:, None] == j, taps_shot[None, :, None, None, j], 0.0)]
    unnamed x41 -> x0, local copies, waits for them, and re-layouts: 3.66 us -> none
    convert_element_type x1 -> x0, other arithmetic: 2.08 us -> none  [filter_matrices(): (time_part * shot_part).astype(jnp.bfloat16).reshape(2, ROWS, COLS)]
    pallas_call x1, Pallas kernels: 3.7 us -> 1.81 us  [unpack(): pl.pallas_call(from_messages, out_shape=jax.ShapeDtypeStruct((REC, TT), j...]
    pallas_call x1, Pallas kernels: 3.43 us -> 1.74 us  [pack(): pl.pallas_call(to_messages, out_shape=(jax.ShapeDtypeStruct((REC * ITEM,...]
  transfers between devices with their start and end apart: 1 -> 0, of which waited for: 1 -> 0; matrix products, arithmetic and copies ran while one was open for 10% -> 0% of each run, Pallas kernels for 0% -> 0%
where the time goes in v2:
time: 88.2 us; the launch traced here: 88 us
  blocking collectives  68.8 us (78%)
  Pallas kernels  18.5 us (21%)
    all_to_all x1, blocking collectives, per_device(): lax.all_to_all(sent, group, split_axis=0, concat_axis=0, tiled=True)  42.1 us
    all_to_all x1, blocking collectives, per_device(): lax.all_to_all(result, group, split_axis=0, concat_axis=0, tiled=True)  26.7 us
    pallas_call x1, Pallas kernels, deblend(): pl.pallas_call(deblend_kernel, out_shape=jax.ShapeDtypeStruct((REC, TILES...  15 us
    pallas_call x1, Pallas kernels, unpack(): pl.pallas_call(from_messages, out_shape=jax.ShapeDtypeStruct((REC, TT), j...  1.81 us

profile of v2, /device:TPU:1, one launch (start us, length us, event | category | flops | bytes accessed | tf_op | source)
XLA Modules:
  0.0 88.0 jit_solution(3216656912423819371)
XLA Ops:
  0.7 1.7 %pack.1 = (bf16[3328,128]{1,0:T(8,128)(2,1)S(1)}, bf16[2,512,256]{2,1,0:T(8,128)(2,1)S(1)}, bf16[2,256,512]{2,1,0:T(8,128)(2,1)S(1)}) custom-call(s32[1]{0:T(128)} %bitcast.half_ref, s32[1]{0:T(128)} %bitcast.9.delay_ref, bf16[128,2048]{1,0:T(8,128)(2,1)} %bitcast.12, bf16[128,2048]{1,0:T(8,128)(2,1)} %bitcast.13, f32[7,16]{1,0:T(8,128)} %bitcast.14, ...), custom_call_target="tpu_custom_call" | custom-call | tf_op jit(solution)/shard_map/pack/pallas_call | solution.py:119
  2.4 42.1 %all_to_all.10 = bf16[128,13,2,128]{3,2,1,0:T(2,128)(2,1)S(1)} all-to-all(bf16[128,13,2,128]{3,2,1,0:T(2,128)(2,1)S(1)} %bitcast.11), channel_id=1, replica_groups=mesh['vessel'=2,'pairs'=64,'parity'=2] {'vessel','pairs'}, dimensions={0} | all-to-all | bytes 1703936 | tf_op jit(solution)/shard_map/all_to_all | solution.py:329
  44.5 15.0 %deblend.1 = bf16[128,16,128]{2,1,0:T(8,128)(2,1)S(1)} custom-call(f32[16]{0:T(128)} %thresh_hbm.1, bf16[3328,128]{1,0:T(8,128)(2,1)S(1)} %bitcast.10, bf16[2,512,256]{2,1,0:T(8,128)(2,1)S(1)} %get-tuple-element.9.fwd_ref, bf16[2,256,512]{2,1,0:T(8,128)(2,1)S(1)} %get-tuple-element.10.bwd_ref), custom_call_target="tpu_custom_call" | custom-call | tf_op jit(solution)/shard_map/deblend/pallas_call | solution.py:296
  59.5 26.7 %all_to_all.11.in_ref = bf16[128,16,128]{2,1,0:T(8,128)(2,1)S(1)} all-to-all(bf16[128,16,128]{2,1,0:T(8,128)(2,1)S(1)} %deblend.1), channel_id=1, replica_groups=mesh['vessel'=2,'pairs'=64,'parity'=2] {'vessel','pairs'}, dimensions={0} | all-to-all | bytes 1048576 | tf_op jit(solution)/shard_map/all_to_all | solution.py:331
  86.2 1.8 %unpack.1 = bf16[128,2048]{1,0:T(8,128)(2,1)} custom-call(bf16[128,16,128]{2,1,0:T(8,128)(2,1)S(1)} %all_to_all.11.in_ref), custom_call_target="tpu_custom_call" | custom-call | tf_op jit(solution)/shard_map/unpack/pallas_call | solution.py:143

commit v3 on v2

--- a/solution.py
+++ b/solution.py
@@ -200,89 +200,106 @@
     lax.fori_loop(0, PAIR // 8, sort_out, 0)
     for slot in slots:
         slot[...] = jnp.zeros_like(slot)
-    wide[:, TT:] = jnp.zeros((PAIR, 128), jnp.float32)
-    spread[:, :, TT:] = jnp.zeros((2, COLS, 128), jnp.float32)
+    wide[:, :, TT:] = jnp.zeros((2, PAIR, 128), jnp.float32)
+    spread[:, :, :, TT:] = jnp.zeros((2, 2, COLS, 128), jnp.float32)
     halo[...] = jnp.zeros_like(halo)
     fetch.wait()
     limits.wait()
 
+    def blend_some(group):
+        for u in range(UNROLL):
+            shot = group * UNROLL + u
+            first, second = delays_ref[0, shot], delays_ref[0, PAIR + shot]
+            at = 4 * (shot % (2 * UNROLL))
+            mine = slots[at : at + 4]
+            a, b = traces[shot], traces[PAIR + shot]
+            resid = observed[shot] - (late(a, first, mine[0], lane) + late(b, second, mine[1], lane))
+            planes[0, shot] = a + early(resid, first, mine[2], lane)
+            planes[1, shot] = b + early(resid, second, mine[3], lane)
+
+    def shift_rows(vessel, g):
+        some = slice(16 * g, 16 * g + 16)
+        for j in range(TILES):
+            wide[vessel, some, 128 * j : 128 * (j + 1)] = planes[vessel, some, j, :]
+        rows = wide[vessel, some, :]
+        block, inner = g // 2, 16 * (g % 2)
+        for k in range(TAPS):
+            moved = rows if k == 3 else pltpu.roll(rows, (STEP * (3 - k)) % WIDE, 1)
+            moved = moved[:, :TT]
+            columns[vessel, block, k * BLOCK + inner : k * BLOCK + inner + 16, :] = moved.astype(jnp.bfloat16)
+            if g == 2:
+                halo[vessel, 0, 4 * k : 4 * k + 4, :] = moved[0:4]
+            if g == 1:
+                halo[vessel, 1, 4 * k : 4 * k + 4, :] = moved[12:16]
+
+    def place_halo(vessel, block):
+        columns[vessel, block, HALO:, :] = halo[vessel, block].astype(jnp.bfloat16)
+
+    def filter_tile(vessel, block, n):
+        at = slice(n * TILE, (n + 1) * TILE)
+        y = jnp.dot(fwd_ref[block], columns[vessel, block, :, at], preferred_element_type=jnp.float32)
+        parts = []
+        for c in range(CH):
+            limit = thresh_ref[c]
+            part = y[BLOCK * c : BLOCK * (c + 1)]
+            parts.append((part - jnp.clip(part, -limit, limit)).astype(jnp.bfloat16))
+        spread[vessel, block, :, at] = jnp.dot(bwd_ref[block], jnp.concatenate(parts, axis=0), preferred_element_type=jnp.float32)
+
+    def gather_rows(vessel, block, g):
+        total = None
+        for k in range(TAPS):
+            part = spread[vessel, block, k * BLOCK + 8 * g : k * BLOCK + 8 * g + 8, :]
+            if k != 3:
+                part = pltpu.roll(part, (STEP * (k - 3)) % WIDE, 1)
+            part = part[:, :TT]
+            total = part if total is None else total + part
+        edge = 3 if block == 0 else 0
+        if g == edge:
+            even = odd = None
+            for m in range(4):
+                pair = spread[vessel, 1 - block, HALO + 8 * m : HALO + 8 * m + 8, :]
+                moved = pltpu.roll(pair, (STEP * (2 * m - 3)) % WIDE, 1)[:, :TT]
+                even = moved if even is None else even + moved
+                if m < 3:
+                    moved = pltpu.roll(pair, (STEP * (2 * m - 2)) % WIDE, 1)[:, :TT]
+                    odd = moved if odd is None else odd + moved
+            if block == 0:
+                total = total + jnp.where(row >= 4, pltpu.roll(even, 4, 0) + odd, 0.0)
+            else:
+                total = total + jnp.where(row < 4, even + pltpu.roll(odd, 4, 0), 0.0)
+        total = total.astype(jnp.bfloat16).astype(jnp.float32)
+        at = vessel * PAIR + block * BLOCK + 8 * g
+        for j in range(TILES):
+            traces[at : at + 8, j, :] = total[:, 128 * j : 128 * (j + 1)]
+
+    def blend(*groups):
+        return [functools.partial(blend_some, group) for group in groups]
+
+    def shift(vessel, *groups):
+        return [functools.partial(shift_rows, vessel, g) for g in groups]
+
+    def join(vessel, block):
+        return [functools.partial(place_halo, vessel, block)]
+
+    def gather(vessel, block, *groups):
+        return [functools.partial(gather_rows, vessel, block, g) for g in groups]
+
+    def beside(vessel, block, jobs):
+        count = TT // TILE
+        for n in range(count):
+            filter_tile(vessel, block, n)
+            for job in jobs[n * len(jobs) // count : (n + 1) * len(jobs) // count]:
+                job()
+
     def one_iteration(_, carry):
-        def blend_some(group, carry):
-            for u in range(UNROLL):
-                shot = group * UNROLL + u
-                first, second = delays_ref[0, shot], delays_ref[0, PAIR + shot]
-                mine = slots[4 * u : 4 * u + 4]
-                a, b = traces[shot], traces[PAIR + shot]
-                resid = observed[shot] - (late(a, first, mine[0], lane) + late(b, second, mine[1], lane))
-                planes[0, shot] = a + early(resid, first, mine[2], lane)
-                planes[1, shot] = b + early(resid, second, mine[3], lane)
-            return carry
-
-        lax.fori_loop(0, PAIR // UNROLL, blend_some, 0)
-
-        def one_vessel(vessel, carry):
-            for j in range(TILES):
-                wide[:, 128 * j : 128 * (j + 1)] = planes[vessel, :, j, :]
-            for g in range(PAIR // 16):
-                rows = wide[16 * g : 16 * g + 16, :]
-                block, inner = g // 2, 16 * (g % 2)
-                for k in range(TAPS):
-                    moved = rows if k == 3 else pltpu.roll(rows, (STEP * (3 - k)) % WIDE, 1)
-                    moved = moved[:, :TT]
-                    columns[block, k * BLOCK + inner : k * BLOCK + inner + 16, :] = moved.astype(jnp.bfloat16)
-                    if g == 2:
-                        halo[0, 4 * k : 4 * k + 4, :] = moved[0:4]
-                    if g == 1:
-                        halo[1, 4 * k : 4 * k + 4, :] = moved[12:16]
-            columns[:, HALO:, :] = halo[...].astype(jnp.bfloat16)
-
-            def one_tile(n, carry):
-                at = pl.ds(pl.multiple_of(n * TILE, TILE), TILE)
-                for block in range(2):
-                    piece = columns[block, :, at]
-                    y = jnp.dot(fwd_ref[block], piece, preferred_element_type=jnp.float32)
-                    for c in range(CH):
-                        limit = thresh_ref[c]
-                        part = y[BLOCK * c : BLOCK * (c + 1)]
-                        z = part - jnp.clip(part, -limit, limit)
-                        shrunk[block, BLOCK * c : BLOCK * (c + 1), :] = z.astype(jnp.bfloat16)
-                    spread[block, :, at] = jnp.dot(
-                        bwd_ref[block], shrunk[block], preferred_element_type=jnp.float32
-                    )
-                return carry
-
-            lax.fori_loop(0, TT // TILE, one_tile, 0, unroll=True)
-
-            for block in range(2):
-                for g in range(BLOCK // 8):
-                    total = None
-                    for k in range(TAPS):
-                        part = spread[block, k * BLOCK + 8 * g : k * BLOCK + 8 * g + 8, :]
-                        if k != 3:
-                            part = pltpu.roll(part, (STEP * (k - 3)) % WIDE, 1)
-                        part = part[:, :TT]
-                        total = part if total is None else total + part
-                    edge = 3 if block == 0 else 0
-                    if g == edge:
-                        even = odd = None
-                        for m in range(4):
-                            pair = spread[1 - block, HALO + 8 * m : HALO + 8 * m + 8, :]
-                            moved = pltpu.roll(pair, (STEP * (2 * m - 3)) % WIDE, 1)[:, :TT]
-                            even = moved if even is None else even + moved
-                            if m < 3:
-                                moved = pltpu.roll(pair, (STEP * (2 * m - 2)) % WIDE, 1)[:, :TT]
-                                odd = moved if odd is None else odd + moved
-                        if block == 0:
-                            total = total + jnp.where(row >= 4, pltpu.roll(even, 4, 0) + odd, 0.0)
-                        else:
-                            total = total + jnp.where(row < 4, even + pltpu.roll(odd, 4, 0), 0.0)
-                    total = total.astype(jnp.bfloat16).astype(jnp.float32)
-                    at = pl.ds(vessel * PAIR + block * BLOCK + 8 * g, 8)
-                    for j in range(TILES):
-                        traces[at, j, :] = total[:, 128 * j : 128 * (j + 1)]
-            return carry
-
-        lax.fori_loop(0, 2, one_vessel, 0, unroll=True)
+        for job in blend(0, 1, 2, 3) + shift(0, 0, 1) + blend(4, 5) + shift(0, 2) + join(0, 0):
+            job()
+        beside(0, 0, blend(6, 7) + shift(0, 3) + join(0, 1) + shift(1, 0, 1))
+        beside(0, 1, shift(1, 2, 3) + join(1, 0) + join(1, 1) + gather(0, 0, 0, 1, 2))
+        beside(1, 0, gather(0, 0, 3) + gather(0, 1, 0, 1, 2, 3))
+        beside(1, 1, gather(1, 0, 0, 1, 2))
+        for job in gather(1, 0, 3) + gather(1, 1, 0, 1, 2, 3):
+            job()
         return carry
 
     lax.fori_loop(0, ITERS, one_iteration, 0)
@@ -307,13 +324,13 @@
             pltpu.VMEM((REC, TILES, 128), f32),
             pltpu.VMEM((PAIR, TILES, 128), f32),
             pltpu.VMEM((2, PAIR, TILES, 128), f32),
-            pltpu.VMEM((PAIR, WIDE), f32),
-            pltpu.VMEM((2, COLS, TT), jnp.bfloat16),
-            pltpu.VMEM((2, BLOCK, TT), f32),
-            pltpu.VMEM((2, ROWS, TILE), jnp.bfloat16),
-            pltpu.VMEM((2, COLS, WIDE), f32),
+            pltpu.VMEM((2, PAIR, WIDE), f32),
+            pltpu.VMEM((2, 2, COLS, TT), jnp.bfloat16),
+            pltpu.VMEM((2, 2, BLOCK, TT), f32),
+            pltpu.VMEM((4, ROWS, TILE), jnp.bfloat16),
+            pltpu.VMEM((2, 2, COLS, WIDE), f32),
         ]
-        + [pltpu.VMEM((24, 128), f32)] * (4 * UNROLL),
+        + [pltpu.VMEM((24, 128), f32)] * (8 * UNROLL),
         compiler_params=pltpu.CompilerParams(vmem_limit_bytes=40 << 20),
         name="deblend",
     )(stay(thresh), messages, forward, backward)

time: 88.2 us -> 86.5 us (0.981)
  Pallas kernels: 18.5 us -> 16.9 us
    pallas_call x1, Pallas kernels: 15 us -> 13.3 us  [deblend(): pl.pallas_call(deblend_kernel, out_shape=jax.ShapeDtypeStruct((REC, TILES...]
where the time goes in v3:
time: 86.5 us; the launch traced here: 86.4 us
  blocking collectives  68.9 us (80%)
  Pallas kernels  16.9 us (20%)
    all_to_all x1, blocking collectives, per_device(): lax.all_to_all(sent, group, split_axis=0, concat_axis=0, tiled=True)  42.1 us
    all_to_all x1, blocking collectives, per_device(): lax.all_to_all(result, group, split_axis=0, concat_axis=0, tiled=True)  26.7 us
    pallas_call x1, Pallas kernels, deblend(): pl.pallas_call(deblend_kernel, out_shape=jax.ShapeDtypeStruct((REC, TILES...  13.3 us
    pallas_call x1, Pallas kernels, unpack(): pl.pallas_call(from_messages, out_shape=jax.ShapeDtypeStruct((REC, TT), j...  1.81 us
    pallas_call x1, Pallas kernels, pack(): pl.pallas_call(to_messages, out_shape=(jax.ShapeDtypeStruct((REC * ITEM,...  1.74 us

profile of v3, /device:TPU:1, one launch (start us, length us, event | category | flops | bytes accessed | tf_op | source)
XLA Modules:
  0.0 86.4 jit_solution(10914406635042454013)
XLA Ops:
  0.7 1.7 %pack.1 = (bf16[3328,128]{1,0:T(8,128)(2,1)S(1)}, bf16[2,512,256]{2,1,0:T(8,128)(2,1)S(1)}, bf16[2,256,512]{2,1,0:T(8,128)(2,1)S(1)}) custom-call(s32[1]{0:T(128)} %bitcast.half_ref, s32[1]{0:T(128)} %bitcast.9.delay_ref, bf16[128,2048]{1,0:T(8,128)(2,1)} %bitcast.12, bf16[128,2048]{1,0:T(8,128)(2,1)} %bitcast.13, f32[7,16]{1,0:T(8,128)} %bitcast.14, ...), custom_call_target="tpu_custom_call" | custom-call | tf_op jit(solution)/shard_map/pack/pallas_call | solution.py:119
  2.4 42.1 %all_to_all.10 = bf16[128,13,2,128]{3,2,1,0:T(2,128)(2,1)S(1)} all-to-all(bf16[128,13,2,128]{3,2,1,0:T(2,128)(2,1)S(1)} %bitcast.11), channel_id=1, replica_groups=mesh['vessel'=2,'pairs'=64,'parity'=2] {'vessel','pairs'}, dimensions={0} | all-to-all | bytes 1703936 | tf_op jit(solution)/shard_map/all_to_all | solution.py:346
  44.5 13.3 %deblend.1 = bf16[128,16,128]{2,1,0:T(8,128)(2,1)S(1)} custom-call(f32[16]{0:T(128)} %thresh_hbm.1, bf16[3328,128]{1,0:T(8,128)(2,1)S(1)} %bitcast.10, bf16[2,512,256]{2,1,0:T(8,128)(2,1)S(1)} %get-tuple-element.9.fwd_ref, bf16[2,256,512]{2,1,0:T(8,128)(2,1)S(1)} %get-tuple-element.10.bwd_ref), custom_call_target="tpu_custom_call" | custom-call | tf_op jit(solution)/shard_map/deblend/pallas_call | solution.py:313
  57.9 26.7 %all_to_all.11.in_ref = bf16[128,16,128]{2,1,0:T(8,128)(2,1)S(1)} all-to-all(bf16[128,16,128]{2,1,0:T(8,128)(2,1)S(1)} %deblend.1), channel_id=1, replica_groups=mesh['vessel'=2,'pairs'=64,'parity'=2] {'vessel','pairs'}, dimensions={0} | all-to-all | bytes 1048576 | tf_op jit(solution)/shard_map/all_to_all | solution.py:348
  84.6 1.8 %unpack.1 = bf16[128,2048]{1,0:T(8,128)(2,1)} custom-call(bf16[128,16,128]{2,1,0:T(8,128)(2,1)S(1)} %all_to_all.11.in_ref), custom_call_target="tpu_custom_call" | custom-call | tf_op jit(solution)/shard_map/unpack/pallas_call | solution.py:143

commit v4 on v3

--- a/solution.py
+++ b/solution.py
@@ -23,7 +23,7 @@
 WIDE = TT + 128
 ITEM = TILES + HALF + 2
 TILE = 256
-PART = 32
+PART = 64
 UNROLL = 8
 
 
@@ -98,9 +98,7 @@
     copies = []
     for part in range(REC // PART):
         rows = pl.ds(PART * part, PART)
-        wide_ref[rows] = in_ref[rows].astype(jnp.float32)
-        for j in range(TILES):
-            out_ref[rows, 128 * j : 128 * (j + 1)] = wide_ref[rows, j, :].astype(jnp.bfloat16)
+        out_ref[rows, :] = in_ref[rows].reshape(PART, TT)
         copies.append(pltpu.make_async_copy(out_ref.at[rows], out_hbm.at[rows], departures.at[part]))
         copies[-1].start()
     for copy in copies:
@@ -219,8 +217,7 @@
 
     def shift_rows(vessel, g):
         some = slice(16 * g, 16 * g + 16)
-        for j in range(TILES):
-            wide[vessel, some, 128 * j : 128 * (j + 1)] = planes[vessel, some, j, :]
+        wide[vessel, some, :TT] = planes[vessel, some].reshape(16, TT)
         rows = wide[vessel, some, :]
         block, inner = g // 2, 16 * (g % 2)
         for k in range(TAPS):
@@ -269,8 +266,7 @@
                 total = total + jnp.where(row < 4, even + pltpu.roll(odd, 4, 0), 0.0)
         total = total.astype(jnp.bfloat16).astype(jnp.float32)
         at = vessel * PAIR + block * BLOCK + 8 * g
-        for j in range(TILES):
-            traces[at : at + 8, j, :] = total[:, 128 * j : 128 * (j + 1)]
+        traces[at : at + 8] = total.reshape(8, TILES, 128)
 
     def blend(*groups):
         return [functools.partial(blend_some, group) for group in groups]

time: 86.5 us -> 84.6 us (0.978)
  Pallas kernels: 16.9 us -> 14.9 us
    pallas_call x1, Pallas kernels: 1.81 us -> 0.9 us  [unpack(): pl.pallas_call(from_messages, out_shape=jax.ShapeDtypeStruct((REC, TT), j...]
    pallas_call x1, Pallas kernels: 13.3 us -> 12.4 us  [deblend(): pl.pallas_call(deblend_kernel, out_shape=jax.ShapeDtypeStruct((REC, TILES...]
where the time goes in v4:
time: 84.6 us; the launch traced here: 84.4 us
  blocking collectives  68.8 us (81%)
  Pallas kernels  14.9 us (18%)
    all_to_all x1, blocking collectives, per_device(): lax.all_to_all(sent, group, split_axis=0, concat_axis=0, tiled=True)  42.1 us
    all_to_all x1, blocking collectives, per_device(): lax.all_to_all(result, group, split_axis=0, concat_axis=0, tiled=True)  26.7 us
    pallas_call x1, Pallas kernels, deblend(): pl.pallas_call(deblend_kernel, out_shape=jax.ShapeDtypeStruct((REC, TILES...  12.4 us

profile of v4, /device:TPU:1, one launch (start us, length us, event | category | flops | bytes accessed | tf_op | source)
XLA Modules:
  0.0 84.4 jit_solution(5740369379768219228)
XLA Ops:
  0.7 1.6 %pack.1 = (bf16[3328,128]{1,0:T(8,128)(2,1)S(1)}, bf16[2,512,256]{2,1,0:T(8,128)(2,1)S(1)}, bf16[2,256,512]{2,1,0:T(8,128)(2,1)S(1)}) custom-call(s32[1]{0:T(128)} %bitcast.half_ref, s32[1]{0:T(128)} %bitcast.9.delay_ref, bf16[128,2048]{1,0:T(8,128)(2,1)} %bitcast.12, bf16[128,2048]{1,0:T(8,128)(2,1)} %bitcast.13, f32[7,16]{1,0:T(8,128)} %bitcast.14, ...), custom_call_target="tpu_custom_call" | custom-call | tf_op jit(solution)/shard_map/pack/pallas_call | solution.py:117
  2.3 42.1 %all_to_all.10 = bf16[128,13,2,128]{3,2,1,0:T(2,128)(2,1)S(1)} all-to-all(bf16[128,13,2,128]{3,2,1,0:T(2,128)(2,1)S(1)} %bitcast.11), channel_id=1, replica_groups=mesh['vessel'=2,'pairs'=64,'parity'=2] {'vessel','pairs'}, dimensions={0} | all-to-all | bytes 1703936 | tf_op jit(solution)/shard_map/all_to_all | solution.py:342
  44.4 12.4 %deblend.1 = bf16[128,16,128]{2,1,0:T(8,128)(2,1)S(1)} custom-call(f32[16]{0:T(128)} %thresh_hbm.1, bf16[3328,128]{1,0:T(8,128)(2,1)S(1)} %bitcast.10, bf16[2,512,256]{2,1,0:T(8,128)(2,1)S(1)} %get-tuple-element.9.fwd_ref, bf16[2,256,512]{2,1,0:T(8,128)(2,1)S(1)} %get-tuple-element.10.bwd_ref), custom_call_target="tpu_custom_call" | custom-call | tf_op jit(solution)/shard_map/deblend/pallas_call | solution.py:309
  56.8 26.7 %all_to_all.11.in_ref = bf16[128,16,128]{2,1,0:T(8,128)(2,1)S(1)} all-to-all(bf16[128,16,128]{2,1,0:T(8,128)(2,1)S(1)} %deblend.1), channel_id=1, replica_groups=mesh['vessel'=2,'pairs'=64,'parity'=2] {'vessel','pairs'}, dimensions={0} | all-to-all | bytes 1048576 | tf_op jit(solution)/shard_map/all_to_all | solution.py:344
  83.5 0.9 %unpack.1 = bf16[128,2048]{1,0:T(8,128)(2,1)} custom-call(bf16[128,16,128]{2,1,0:T(8,128)(2,1)S(1)} %all_to_all.11.in_ref), custom_call_target="tpu_custom_call" | custom-call | tf_op jit(solution)/shard_map/unpack/pallas_call | solution.py:141

commit v5 on v4

--- a/solution.py
+++ b/solution.py
@@ -171,7 +171,7 @@
 
 def deblend_kernel(
     thresh_hbm, recv_ref, fwd_ref, bwd_ref, out_ref,
-    thresh_ref, arrived, delay_row, delays_ref, arrivals, traces, observed, planes, wide, columns, halo, shrunk, spread, *slots
+    thresh_ref, arrived, delay_row, delays_ref, arrivals, traces, observed, wide, columns, halo, shrunk, spread, *slots
 ):
     lane = lax.broadcasted_iota(jnp.int32, (TILES, 128), 1)
     row = lax.broadcasted_iota(jnp.int32, (8, TT), 0)
@@ -205,6 +205,7 @@
     limits.wait()
 
     def blend_some(group):
+        made = ([], [])
         for u in range(UNROLL):
             shot = group * UNROLL + u
             first, second = delays_ref[0, shot], delays_ref[0, PAIR + shot]
@@ -212,12 +213,14 @@
             mine = slots[at : at + 4]
             a, b = traces[shot], traces[PAIR + shot]
             resid = observed[shot] - (late(a, first, mine[0], lane) + late(b, second, mine[1], lane))
-            planes[0, shot] = a + early(resid, first, mine[2], lane)
-            planes[1, shot] = b + early(resid, second, mine[3], lane)
+            made[0].append(a + early(resid, first, mine[2], lane))
+            made[1].append(b + early(resid, second, mine[3], lane))
+        some = slice(group * UNROLL, (group + 1) * UNROLL)
+        for vessel in range(2):
+            wide[vessel, some, :TT] = jnp.stack(made[vessel]).reshape(UNROLL, TT)
 
     def shift_rows(vessel, g):
         some = slice(16 * g, 16 * g + 16)
-        wide[vessel, some, :TT] = planes[vessel, some].reshape(16, TT)
         rows = wide[vessel, some, :]
         block, inner = g // 2, 16 * (g % 2)
         for k in range(TAPS):
@@ -319,7 +322,6 @@
             pltpu.SemaphoreType.DMA((2,)),
             pltpu.VMEM((REC, TILES, 128), f32),
             pltpu.VMEM((PAIR, TILES, 128), f32),
-            pltpu.VMEM((2, PAIR, TILES, 128), f32),
             pltpu.VMEM((2, PAIR, WIDE), f32),
             pltpu.VMEM((2, 2, COLS, TT), jnp.bfloat16),
             pltpu.VMEM((2, 2, BLOCK, TT), f32),

time: 84.6 us -> 84.5 us (level)
  no operation moved by 1% of the time
where the time goes in v5:
time: 84.5 us; the launch traced here: 84.3 us
  blocking collectives  68.8 us (81%)
  Pallas kernels  14.9 us (18%)
    all_to_all x1, blocking collectives, per_device(): lax.all_to_all(sent, group, split_axis=0, concat_axis=0, tiled=True)  42.1 us
    all_to_all x1, blocking collectives, per_device(): lax.all_to_all(result, group, split_axis=0, concat_axis=0, tiled=True)  26.7 us
    pallas_call x1, Pallas kernels, deblend(): pl.pallas_call(deblend_kernel, out_shape=jax.ShapeDtypeStruct((REC, TILES...  12.4 us

profile of v5, /device:TPU:1, one launch (start us, length us, event | category | flops | bytes accessed | tf_op | source)
XLA Modules:
  0.0 84.3 jit_solution(969461026403180352)
XLA Ops:
  0.7 1.6 %pack.1 = (bf16[3328,128]{1,0:T(8,128)(2,1)S(1)}, bf16[2,512,256]{2,1,0:T(8,128)(2,1)S(1)}, bf16[2,256,512]{2,1,0:T(8,128)(2,1)S(1)}) custom-call(s32[1]{0:T(128)} %bitcast.half_ref, s32[1]{0:T(128)} %bitcast.9.delay_ref, bf16[128,2048]{1,0:T(8,128)(2,1)} %bitcast.12, bf16[128,2048]{1,0:T(8,128)(2,1)} %bitcast.13, f32[7,16]{1,0:T(8,128)} %bitcast.14, ...), custom_call_target="tpu_custom_call" | custom-call | tf_op jit(solution)/shard_map/pack/pallas_call | solution.py:117
  2.3 42.1 %all_to_all.10 = bf16[128,13,2,128]{3,2,1,0:T(2,128)(2,1)S(1)} all-to-all(bf16[128,13,2,128]{3,2,1,0:T(2,128)(2,1)S(1)} %bitcast.11), channel_id=1, replica_groups=mesh['vessel'=2,'pairs'=64,'parity'=2] {'vessel','pairs'}, dimensions={0} | all-to-all | bytes 1703936 | tf_op jit(solution)/shard_map/all_to_all | solution.py:344
  44.4 12.4 %deblend.1 = bf16[128,16,128]{2,1,0:T(8,128)(2,1)S(1)} custom-call(f32[16]{0:T(128)} %thresh_hbm.1, bf16[3328,128]{1,0:T(8,128)(2,1)S(1)} %bitcast.10, bf16[2,512,256]{2,1,0:T(8,128)(2,1)S(1)} %get-tuple-element.9.fwd_ref, bf16[2,256,512]{2,1,0:T(8,128)(2,1)S(1)} %get-tuple-element.10.bwd_ref), custom_call_target="tpu_custom_call" | custom-call | tf_op jit(solution)/shard_map/deblend/pallas_call | solution.py:312
  56.8 26.7 %all_to_all.11.in_ref = bf16[128,16,128]{2,1,0:T(8,128)(2,1)S(1)} all-to-all(bf16[128,16,128]{2,1,0:T(8,128)(2,1)S(1)} %deblend.1), channel_id=1, replica_groups=mesh['vessel'=2,'pairs'=64,'parity'=2] {'vessel','pairs'}, dimensions={0} | all-to-all | bytes 1048576 | tf_op jit(solution)/shard_map/all_to_all | solution.py:346
  83.4 0.9 %unpack.1 = bf16[128,2048]{1,0:T(8,128)(2,1)} custom-call(bf16[128,16,128]{2,1,0:T(8,128)(2,1)S(1)} %all_to_all.11.in_ref), custom_call_target="tpu_custom_call" | custom-call | tf_op jit(solution)/shard_map/unpack/pallas_call | solution.py:141
